TPU v7x, 512 devices: a whole 4x4x16 slice. The times are simulated.
512 devices in a mesh: mp: 2 (over y_hi), tok: 8 (over x, core), lat: 32 (over z, y_lo).
Axes of the slice: x: 4, y: 4 (y_hi: 2, y_lo: 2; y = y_hi * 2 + y_lo), z: 16, core: 2. Of those that a mesh axis runs over, the one named last changes fastest.
Arguments:
- inputs: bfloat16 [2, 384, 4608], P('mp', 'lat', 'tok'), may hold values from -6 to 6
- gate_w: bfloat16 [2, 4608, 18432], P('mp', 'tok', 'lat'), may hold values from -0.09375 to 0.09375
- up_w: bfloat16 [2, 4608, 18432], P('mp', 'tok', 'lat'), may hold values from -0.09375 to 0.09375
- down_w: bfloat16 [2, 18432, 4608], P('mp', 'lat', 'tok'), may hold values from -0.046875 to 0.046875
- enc_w: bfloat16 [2, 4608, 8192], P('mp', 'tok', 'lat'), may hold values from -0.0625 to 0.0625
- enc_bias: float32 [8192], P('lat'), may hold values from -3 to 3
- dec_w: bfloat16 [8192, 2, 4608], P('lat', 'mp', 'tok'), may hold values from -0.0625 to 0.0625
- dec_bias: float32 [2, 4608], P('mp', 'tok'), may hold values from -3 to 3
Outputs:
- recon_error: float32 [2, 384, 4608], P('mp', 'lat', 'tok')
- dec_grad: float32 [8192, 2, 4608], P('lat', 'mp', 'tok')
- latent_grad: float32 [384, 8192], P(None, 'lat')
All inputs are finite; a program needn't handle non-finite values.
Results may differ from a plain program's by a relative error of at most 0.009.
Values may be sent and summed in bfloat16 or wider, within the bound.
A program may use at most 64 MiB of HBM per device.

v0:
```python
import jax
import jax.numpy as jnp
from jax import lax
from jax.sharding import PartitionSpec as P


def contract_rows(left, right):
    return lax.dot_general(
        left, right, (((0,), (0,)), ((), ())), preferred_element_type=jnp.float32
    )


def contract_cols(left, right):
    return lax.dot_general(
        left, right, (((1,), (1,)), ((), ())), preferred_element_type=jnp.float32
    )


def body(inputs, gate_w, up_w, down_w, enc_w, enc_bias, dec_w, dec_bias):
    x_rows = inputs[0]
    gathered = lax.all_gather(x_rows, "lat", axis=0, tiled=True)
    gate_local = gate_w[0]
    up_local = up_w[0]
    width = gate_local.shape[1]
    block = gathered
    both = lax.psum_scatter(
        jnp.concatenate(
            [
                jnp.dot(block, gate_local, preferred_element_type=jnp.float32),
                jnp.dot(block, up_local, preferred_element_type=jnp.float32),
            ],
            axis=1,
        ),
        "tok",
        scatter_dimension=0,
        tiled=True,
    )
    hidden = (jax.nn.gelu(both[:, :width], approximate=True) * both[:, width:]).astype(jnp.bfloat16)
    hidden_all = lax.all_gather(hidden, "tok", axis=0, tiled=True)
    down_local = down_w[0]
    block = hidden_all
    acts = lax.psum_scatter(
        jnp.dot(block, down_local, preferred_element_type=jnp.float32),
        "lat",
        scatter_dimension=0,
        tiled=True,
    ).astype(jnp.bfloat16)
    acts_all = lax.all_gather(acts, "lat", axis=0, tiled=True)
    partial_pre = jnp.dot(acts_all, enc_w[0], preferred_element_type=jnp.float32)
    pre = lax.psum(partial_pre, ("mp", "tok"))
    codes = jnp.maximum(pre + enc_bias, 0.0).astype(jnp.bfloat16)
    decoder = dec_w[:, 0, :]
    bias_row = dec_bias[0]
    block = codes
    recon = lax.psum_scatter(
        jnp.dot(block, decoder, preferred_element_type=jnp.float32),
        "lat",
        scatter_dimension=0,
        tiled=True,
    )
    error = recon + bias_row - acts.astype(jnp.float32)
    error_all = lax.all_gather(error.astype(jnp.bfloat16), "lat", axis=0, tiled=True)
    decoder_grad = contract_rows(codes, error_all)
    latent_grad = lax.psum(contract_cols(error_all, decoder), ("mp", "tok"))
    return (error[None], decoder_grad[:, None, :], latent_grad)


def solution(mesh):
    in_specs = (
        P("mp", "lat", "tok"),
        P("mp", "tok", "lat"),
        P("mp", "tok", "lat"),
        P("mp", "lat", "tok"),
        P("mp", "tok", "lat"),
        P("lat"),
        P("lat", "mp", "tok"),
        P("mp", "tok"),
    )
    out_specs = (P("mp", "lat", "tok"), P("lat", "mp", "tok"), P(None, "lat"))
    return jax.shard_map(body, mesh=mesh, in_specs=in_specs, out_specs=out_specs, check_vma=False)
```

profile of v0, /device:TPU:1, one launch (start us, length us, event | category | flops | bytes accessed | tf_op | source)
XLA Modules:
  0.0 789.7 jit_solution(4947730989583786598)
XLA Ops:
  7.2 0.0 copy-start
  7.2 0.0 reduce-scatter.8.cloned.1.call-start
  7.2 0.8 copy.20
  8.0 61.9 %all-gather = bf16[1,384,576]{2,0,1:T(2,128)(2,1)S(1)} all-gather(bf16[1,12,576]{2,0,1:T(2,128)(2,1)S(1)} %copy.20), channel_id=2, replica_groups=mesh['mp'=2,'tok'=8,'lat'=32] {'lat'}, dimensions={1}, use_global_device_ids=true | all-gather | bytes 456192 | tf_op jit(solution)/shard_map/all_gather | solution.py:21
  70.0 0.7 copy.21
  70.6 0.6 fusion.4
  71.3 0.6 fusion.6
  71.9 0.1 pad_maximum_fusion
  72.1 2.0 copy.25
  74.0 0.0 reduce-scatter.8.cloned.1.call-update
  74.1 0.0 all-reduce.7.cloned.1.call-start
  74.1 47.7 %reduce-scatter.8.cloned.1.call-done = f32[48,1152]{1,0:T(8,128)} async-done(((f32[384,1152]{1,0:T(8,128)}), f32[48,1152]{1,0:T(8,128)}) %reduce-scatter.8.cloned.1.call-update) | async-done | bytes 221200 | tf_op jit(solution)/shard_map/reduce_scatter | solution.py:26
  121.8 1.1 fusion.24
  122.9 15.4 %all_gather.13 = bf16[384,576]{1,0:T(8,128)(2,1)S(1)} all-gather(bf16[48,576]{1,0:T(8,128)(2,1)S(1)} %fusion.24), channel_id=1, replica_groups=mesh['mp'=2,'tok'=8,'lat'=32] {'tok'}, dimensions={0}, use_global_device_ids=true | all-gather | bytes 497664 | tf_op jit(solution)/shard_map/all_gather | solution.py:39
  138.2 0.6 fusion.2
  138.8 0.0 copy-start.5
  138.8 59.0 %fusion = f32[16,576]{1,0:T(8,128)S(1)} fusion(f32[384,576]{1,0:T(8,128)S(1)} %fusion.2), kind=kCustom, calls=%all-reduce-scatter | all-reduce-scatter fusion | flops 294913 | bytes 923648
  197.9 1.7 collective-permute-start
  199.6 2.1 collective-permute-start.1
  201.7 6.0 collective-permute-start.7
  207.7 4.9 collective-permute-start.2
  212.7 4.9 collective-permute-start.3
  217.6 0.0 collective-permute-done.7
  217.6 2.1 collective-permute-start.4
  219.8 3.5 collective-permute-start.5
  223.2 0.0 collective-permute-done.1
  223.2 2.8 collective-permute-start.6
  226.1 1.3 dynamic-slice.6
  228.0 0.0 collective-permute-done.2
  228.0 0.0 collective-permute-done.4
  228.0 0.0 collective-permute-done.5
  228.1 1.3 concatenate.4
  229.4 0.0 copy-start.2
  229.4 0.0 copy-start.6
  229.4 49.4 %all-gather.1 = bf16[32,12,576]{2,1,0:T(8,128)(2,1)S(1)} all-gather(bf16[1,12,576]{2,1,0:T(8,128)(2,1)S(1)} %fusion.31), channel_id=1, replica_groups=mesh['mp'=2,'tok'=8,'lat'=32] {'lat'}, dimensions={0}, use_global_device_ids=true | all-gather | bytes 456192 | tf_op jit(solution)/shard_map/all_gather | solution.py:48
  278.8 0.2 reshape.9
  279.1 1.1 fusion.14
  280.2 0.0 all-reduce.7.cloned.1.call-update
  280.2 0.0 all-reduce.9.cloned.1.call-start
  280.2 180.0 %all-reduce.7.cloned.1.call-done = f32[384,256]{1,0:T(8,128)} async-done(((f32[384,256]{1,0:T(8,128)}), f32[384,256]{1,0:T(8,128)}) %all-reduce.7.cloned.1.call-update) | async-done | bytes 393232 | tf_op jit(solution)/shard_map/psum | solution.py:50
  460.2 1.3 fusion.12
  461.6 59.2 %fusion.1 = f32[16,576]{1,0:T(8,128)S(1)} fusion(f32[384,576]{1,0:T(8,128)S(1)} %fusion.12), kind=kCustom, calls=%all-reduce-scatter.1 | all-reduce-scatter fusion | flops 294913 | bytes 923648
  520.7 1.3 collective-permute-start.10
  522.0 3.4 collective-permute-start.11
  525.5 7.0 collective-permute-start.15
  532.6 4.5 collective-permute-start.12
  537.1 3.9 collective-permute-start.13
  541.0 0.0 collective-permute-done.15
  541.0 2.9 collective-permute-start.14
  543.9 0.0 collective-permute-done.10
  543.9 3.1 collective-permute-start.8
  547.0 2.2 collective-permute-start.9
  549.2 0.0 collective-permute-done.12
  549.3 0.0 collective-permute-done.14
  549.3 1.0 collective-permute-done.9
  550.3 1.0 concatenate.5
  551.3 48.9 %all-gather.2 = bf16[32,12,576]{2,1,0:T(8,128)(2,1)S(1)} all-gather(bf16[1,12,576]{2,1,0:T(8,128)(2,1)S(1)} %get-tuple-element.18), channel_id=1, replica_groups=mesh['mp'=2,'tok'=8,'lat'=32] {'lat'}, dimensions={0}, use_global_device_ids=true | all-gather | bytes 456192 | tf_op jit(solution)/shard_map/all_gather | solution.py:62
  600.2 0.2 reshape.11
  600.4 1.1 fusion.10
  601.5 0.0 all-reduce.9.cloned.1.call-update
  601.5 0.6 copy.24
  602.2 1.2 convolution_bitcast_fusion
  603.3 178.1 %all-reduce.9.cloned.1.call-done = f32[384,256]{1,0:T(8,128)} async-done(((f32[384,256]{1,0:T(8,128)}), f32[384,256]{1,0:T(8,128)}) %all-reduce.9.cloned.1.call-update) | async-done | bytes 393232 | tf_op jit(solution)/shard_map/psum | solution.py:64
  781.4 1.8 copy.29
  (24 shorter events, 0.1 us)
Async XLA Ops:
  7.2 63.5 %copy-start = (bf16[1,576,576]{2,1,0:T(8,128)(2,1)S(1)}, bf16[1,576,576]{2,1,0:T(8,128)(2,1)}, u32[]{:S(2)}) copy-start(bf16[1,576,576]{2,1,0:T(8,128)(2,1)} %param.10) | copy-start | bytes 1990660
  7.2 114.6 %reduce-scatter.8.cloned.1.call-start = ((), (), s32[]{:S(2)}) async-start(), calls=%async_computation.3 | async-start | bytes 1990656 | tf_op jit(solution)/shard_map/reduce_scatter | solution.py:26
  70.0 1.3 copy-start.3
  74.0 64.2 %copy-start.4 = (bf16[1,576,576]{2,1,0:T(8,128)(2,1)S(1)}, bf16[1,576,576]{2,1,0:T(8,128)(2,1)}, u32[]{:S(2)}) copy-start(bf16[1,576,576]{2,1,0:T(8,128)(2,1)} %param.11) | copy-start | bytes 1990660
  74.1 386.2 %all-reduce.7.cloned.1.call-start = ((), (), s32[]{:S(2)}) async-start(), calls=%async_computation.1 | async-start | bytes 786432 | tf_op jit(solution)/shard_map/psum | solution.py:50
  138.8 140.3 %copy-start.5 = (bf16[1,576,256]{2,1,0:T(8,128)(2,1)S(1)}, bf16[1,576,256]{2,1,0:T(8,128)(2,1)}, u32[]{:S(2)}) copy-start(bf16[1,576,256]{2,1,0:T(8,128)(2,1)} %param.12) | copy-start | bytes 884740
  197.9 21.9 %collective-permute-start = (bf16[16,576]{1,0:T(8,128)(2,1)S(1)}, bf16[16,576]{1,0:T(8,128)(2,1)S(1)}, u32[]{:S(2)}, u32[]{:S(2)}) collective-permute-start(bf16[16,576]{1,0:T(8,128)(2,1)S(1)} %convert.14), channel_id=1, source_target_pairs={{0,1},{1,2},{2,3},{3,4},{4,5},{5,6},{6,7},{7,8},{8,9},{9,10},{10,1... | collective-permute-start | bytes 55304
  199.6 23.6 %collective-permute-start.1 = (bf16[16,576]{1,0:T(8,128)(2,1)S(1)}, bf16[16,576]{1,0:T(8,128)(2,1)S(1)}, u32[]{:S(2)}, u32[]{:S(2)}) collective-permute-start(bf16[16,576]{1,0:T(8,128)(2,1)S(1)} %convert.14), channel_id=1, source_target_pairs={{0,2},{1,3},{2,4},{3,5},{4,6},{5,7},{6,8},{7,9},{8,10},{9,11},{10,... | collective-permute-start | bytes 55304
  201.7 15.9 %collective-permute-start.7 = (bf16[12,576]{1,0:T(8,128)(2,1)S(1)}, bf16[12,576]{1,0:T(8,128)(2,1)S(1)}, u32[]{:S(2)}, u32[]{:S(2)}) collective-permute-start(bf16[12,576]{1,0:T(8,128)(2,1)S(1)} %slice.10), channel_id=1, source_target_pairs={{0,8},{1,9},{2,10},{3,11},{4,12},{5,13},{6,14},{7,15},{8,16},{9,17... | collective-permute-start | bytes 41480
  207.7 20.3 %collective-permute-start.2 = (bf16[16,576]{1,0:T(8,128)(2,1)S(1)}, bf16[16,576]{1,0:T(8,128)(2,1)S(1)}, u32[]{:S(2)}, u32[]{:S(2)}) collective-permute-start(bf16[16,576]{1,0:T(8,128)(2,1)S(1)} %convert.14), channel_id=1, source_target_pairs={{0,3},{1,4},{2,5},{3,6},{4,7},{5,8},{6,9},{7,10},{8,11},{9,12},{10... | collective-permute-start | bytes 55304
  212.7 15.3 %collective-permute-start.3 = (bf16[16,576]{1,0:T(8,128)(2,1)S(1)}, bf16[16,576]{1,0:T(8,128)(2,1)S(1)}, u32[]{:S(2)}, u32[]{:S(2)}) collective-permute-start(bf16[16,576]{1,0:T(8,128)(2,1)S(1)} %convert.14), channel_id=1, source_target_pairs={{0,4},{1,5},{2,6},{3,7},{4,8},{5,9},{6,10},{7,11},{8,12},{9,13},{1... | collective-permute-start | bytes 55304
  217.6 10.4 %collective-permute-start.4 = (bf16[16,576]{1,0:T(8,128)(2,1)S(1)}, bf16[16,576]{1,0:T(8,128)(2,1)S(1)}, u32[]{:S(2)}, u32[]{:S(2)}) collective-permute-start(bf16[16,576]{1,0:T(8,128)(2,1)S(1)} %convert.14), channel_id=1, source_target_pairs={{0,5},{1,6},{2,7},{3,8},{4,9},{5,10},{6,11},{7,12},{8,13},{9,14},{... | collective-permute-start | bytes 55304
  219.8 8.3 %collective-permute-start.5 = (bf16[16,576]{1,0:T(8,128)(2,1)S(1)}, bf16[16,576]{1,0:T(8,128)(2,1)S(1)}, u32[]{:S(2)}, u32[]{:S(2)}) collective-permute-start(bf16[16,576]{1,0:T(8,128)(2,1)S(1)} %convert.14), channel_id=1, source_target_pairs={{0,6},{1,7},{2,8},{3,9},{4,10},{5,11},{6,12},{7,13},{8,14},{9,15},... | collective-permute-start | bytes 55304
  223.2 4.8 collective-permute-start.6
  229.4 230.8 %copy-start.2 = (bf16[256,1,576]{0,2,1:T(8,128)(2,1)S(1)}, bf16[256,1,576]{0,2,1:T(8,128)(2,1)}, u32[]{:S(2)}) copy-start(bf16[256,1,576]{0,2,1:T(8,128)(2,1)} %param.14) | copy-start | bytes 884740
  229.4 230.8 %copy-start.6 = (f32[256]{0:T(256)S(1)}, f32[256]{0:T(256)}, u32[]{:S(2)}) copy-start(f32[256]{0:T(256)} %param.13) | copy-start | bytes 3076
  280.2 269.0 %copy-start.7 = (f32[1,576]{1,0:T(1,128)S(1)}, f32[1,576]{1,0:T(1,128)}, u32[]{:S(2)}) copy-start(f32[1,576]{1,0:T(1,128)} %param.15) | copy-start | bytes 6916
  280.2 501.2 %all-reduce.9.cloned.1.call-start = ((), (), s32[]{:S(2)}) async-start(), calls=%async_computation.2 | async-start | bytes 786432 | tf_op jit(solution)/shard_map/psum | solution.py:64
  520.7 23.1 %collective-permute-start.10 = (f32[16,576]{1,0:T(8,128)S(1)}, f32[16,576]{1,0:T(8,128)S(1)}, u32[]{:S(2)}, u32[]{:S(2)}) collective-permute-start(f32[16,576]{1,0:T(8,128)S(1)} %fusion.1), channel_id=1, source_target_pairs={{0,3},{1,4},{2,5},{3,6},{4,7},{5,8},{6,9},{7,10},{8,11},{9,12},{10... | collective-permute-start | bytes 110600
  522.0 24.9 %collective-permute-start.11 = (f32[16,576]{1,0:T(8,128)S(1)}, f32[16,576]{1,0:T(8,128)S(1)}, u32[]{:S(2)}, u32[]{:S(2)}) collective-permute-start(f32[16,576]{1,0:T(8,128)S(1)} %fusion.1), channel_id=1, source_target_pairs={{0,4},{1,5},{2,6},{3,7},{4,8},{5,9},{6,10},{7,11},{8,12},{9,13},{1... | collective-permute-start | bytes 110600
  525.5 15.5 %collective-permute-start.15 = (f32[12,576]{1,0:T(8,128)S(1)}, f32[12,576]{1,0:T(8,128)S(1)}, u32[]{:S(2)}, u32[]{:S(2)}) collective-permute-start(f32[12,576]{1,0:T(8,128)S(1)} %slice.11), channel_id=1, source_target_pairs={{0,8},{1,9},{2,10},{3,11},{4,12},{5,13},{6,14},{7,15},{8,16},{9,17... | collective-permute-start | bytes 82952
  532.6 16.7 %collective-permute-start.12 = (f32[16,576]{1,0:T(8,128)S(1)}, f32[16,576]{1,0:T(8,128)S(1)}, u32[]{:S(2)}, u32[]{:S(2)}) collective-permute-start(f32[16,576]{1,0:T(8,128)S(1)} %fusion.1), channel_id=1, source_target_pairs={{0,5},{1,6},{2,7},{3,8},{4,9},{5,10},{6,11},{7,12},{8,13},{9,14},{... | collective-permute-start | bytes 110600
  537.1 12.2 %collective-permute-start.13 = (f32[16,576]{1,0:T(8,128)S(1)}, f32[16,576]{1,0:T(8,128)S(1)}, u32[]{:S(2)}, u32[]{:S(2)}) collective-permute-start(f32[16,576]{1,0:T(8,128)S(1)} %fusion.1), channel_id=1, source_target_pairs={{0,6},{1,7},{2,8},{3,9},{4,10},{5,11},{6,12},{7,13},{8,14},{9,15},... | collective-permute-start | bytes 110600
  541.0 8.2 %collective-permute-start.14 = (f32[16,576]{1,0:T(8,128)S(1)}, f32[16,576]{1,0:T(8,128)S(1)}, u32[]{:S(2)}, u32[]{:S(2)}) collective-permute-start(f32[16,576]{1,0:T(8,128)S(1)} %fusion.1), channel_id=1, source_target_pairs={{0,7},{1,8},{2,9},{3,10},{4,11},{5,12},{6,13},{7,14},{8,15},{9,16}... | collective-permute-start | bytes 110600
  543.9 5.4 collective-permute-start.8
  547.0 3.3 collective-permute-start.9
  551.3 50.8 %copy-start.1 = (f32[384,256]{1,0:T(8,128)S(1)}, f32[384,256]{1,0:T(8,128)}, u32[]{:S(2)}) copy-start(f32[384,256]{1,0:T(8,128)} %all-reduce.7.cloned.1.call-done) | copy-start | bytes 1179652
Sparse Core Ops, SparseCore 0:
  74.2 47.5 reduce-scatter.7
  280.3 179.8 all-reduce.6
  601.6 179.7 all-reduce.8
where the time goes:
time: 790 us
  waiting for transfers between devices  407 us (52%)
  blocking collectives  294 us (37%)
  starting transfers between devices  56.6 us (7%)
  between operations  14.9 us (2%)
  local copies, waits for them, and re-layouts  10 us (1%)
    psum x1, waiting for transfers between devices, body(): pre = lax.psum(partial_pre, ('mp', 'tok'))  180 us
    psum x1, waiting for transfers between devices, body(): latent_grad = lax.psum(contract_cols(error_all, decoder), ('mp', 'tok'))  178 us
    unnamed x2, blocking collectives  118 us
    all_gather x1, blocking collectives, body(): gathered = lax.all_gather(x_rows, 'lat', axis=0, tiled=True)  61.9 us
    unnamed x16, starting transfers between devices  56.5 us
    all_gather x1, blocking collectives, body(): acts_all = lax.all_gather(acts, 'lat', axis=0, tiled=True)  49.4 us
    all_gather x1, blocking collectives, body(): lax.all_gather(error.astype(jnp.bfloat16), 'lat', axis=0, tiled=True)  48.9 us
    reduce_scatter x1, waiting for transfers between devices, body(): lax.psum_scatter(jnp.concatenate([jnp.dot(block, gate_local, preferred_el...  47.7 us
  transfers between devices with their start and end apart: 19, of which 4 were waited for; matrix products, arithmetic and copies ran while one was open for 0% of the time, Pallas kernels for 0%

commit v1 on v0

--- a/solution.py
+++ b/solution.py
@@ -47,7 +47,7 @@
     ).astype(jnp.bfloat16)
     acts_all = lax.all_gather(acts, "lat", axis=0, tiled=True)
     partial_pre = jnp.dot(acts_all, enc_w[0], preferred_element_type=jnp.float32)
-    pre = lax.psum(partial_pre, ("mp", "tok"))
+    pre = jnp.sum(lax.all_gather(partial_pre, ("mp", "tok")), axis=0)
     codes = jnp.maximum(pre + enc_bias, 0.0).astype(jnp.bfloat16)
     decoder = dec_w[:, 0, :]
     bias_row = dec_bias[0]

time: 790 us -> 716 us (0.906)
  waiting for transfers between devices: 407 us -> 331 us
    psum x1 -> x0, waiting for transfers between devices: 180 us -> none  [body(): pre = lax.psum(partial_pre, ('mp', 'tok'))]
    all_gather x0 -> x1, waiting for transfers between devices: none -> 106 us  [body(): pre = jnp.sum(lax.all_gather(partial_pre, ('mp', 'tok')), axis=0)]
where the time goes in v1:
time: 716 us
  waiting for transfers between devices  331 us (46%)
  blocking collectives  294 us (41%)
  starting transfers between devices  56.3 us (8%)
  between operations  14.9 us (2%)
  local copies, waits for them, and re-layouts  9.99 us (1%)
    psum x1, waiting for transfers between devices, body(): latent_grad = lax.psum(contract_cols(error_all, decoder), ('mp', 'tok'))  176 us
    unnamed x2, blocking collectives  118 us
    all_gather x1, waiting for transfers between devices, body(): pre = jnp.sum(lax.all_gather(partial_pre, ('mp', 'tok')), axis=0)  106 us
    all_gather x1, blocking collectives, body(): gathered = lax.all_gather(x_rows, 'lat', axis=0, tiled=True)  61.9 us
    unnamed x16, starting transfers between devices  56.2 us
    all_gather x1, blocking collectives, body(): acts_all = lax.all_gather(acts, 'lat', axis=0, tiled=True)  49.3 us
    all_gather x1, blocking collectives, body(): lax.all_gather(error.astype(jnp.bfloat16), 'lat', axis=0, tiled=True)  48.9 us
    reduce_scatter x1, waiting for transfers between devices, body(): lax.psum_scatter(jnp.concatenate([jnp.dot(block, gate_local, preferred_el...  47.7 us
  transfers between devices with their start and end apart: 19, of which 4 were waited for; matrix products, arithmetic and copies ran while one was open for 0% of the time, Pallas kernels for 0%

profile of v1, /device:TPU:1, one launch (start us, length us, event | category | flops | bytes accessed | tf_op | source)
XLA Modules:
  0.0 715.7 jit_solution(12954005024369496793)
XLA Ops:
  7.2 0.0 copy-start
  7.2 0.0 reduce-scatter.8.cloned.1.call-start
  7.2 0.8 copy.20
  8.0 61.9 %all-gather = bf16[1,384,576]{2,0,1:T(2,128)(2,1)S(1)} all-gather(bf16[1,12,576]{2,0,1:T(2,128)(2,1)S(1)} %copy.20), channel_id=2, replica_groups=mesh['mp'=2,'tok'=8,'lat'=32] {'lat'}, dimensions={1}, use_global_device_ids=true | all-gather | bytes 456192 | tf_op jit(solution)/shard_map/all_gather | solution.py:21
  70.0 0.7 copy.21
  70.6 0.6 fusion.4
  71.3 0.6 fusion.6
  71.9 0.1 pad_maximum_fusion
  72.1 2.0 copy.25
  74.0 0.0 reduce-scatter.8.cloned.1.call-update
  74.1 0.0 all-gather.6.cloned.1.call-start
  74.1 47.7 %reduce-scatter.8.cloned.1.call-done = f32[48,1152]{1,0:T(8,128)} async-done(((f32[384,1152]{1,0:T(8,128)}), f32[48,1152]{1,0:T(8,128)}) %reduce-scatter.8.cloned.1.call-update) | async-done | bytes 221200 | tf_op jit(solution)/shard_map/reduce_scatter | solution.py:26
  121.8 1.1 fusion.24
  122.8 15.4 %all_gather.19 = bf16[384,576]{1,0:T(8,128)(2,1)S(1)} all-gather(bf16[48,576]{1,0:T(8,128)(2,1)S(1)} %fusion.24), channel_id=1, replica_groups=mesh['mp'=2,'tok'=8,'lat'=32] {'tok'}, dimensions={0}, use_global_device_ids=true | all-gather | bytes 497664 | tf_op jit(solution)/shard_map/all_gather | solution.py:39
  138.2 0.6 fusion.2
  138.8 0.0 copy-start.4
  138.9 58.9 %fusion = f32[16,576]{1,0:T(8,128)S(1)} fusion(f32[384,576]{1,0:T(8,128)S(1)} %fusion.2), kind=kCustom, calls=%all-reduce-scatter | all-reduce-scatter fusion | flops 294913 | bytes 923648
  197.8 2.0 collective-permute-start
  199.8 1.8 collective-permute-start.1
  201.6 5.8 collective-permute-start.7
  207.4 5.1 collective-permute-start.2
  212.5 5.1 collective-permute-start.3
  217.6 0.0 collective-permute-done.7
  217.7 2.1 collective-permute-start.4
  219.8 0.0 collective-permute-done
  219.8 3.4 collective-permute-start.5
  223.2 0.0 collective-permute-done.1
  223.2 2.8 collective-permute-start.6
  226.1 1.3 dynamic-slice.6
  228.0 0.0 collective-permute-done.2
  228.0 0.0 collective-permute-done.3
  228.0 0.0 collective-permute-done.4
  228.0 0.0 collective-permute-done.5
  228.1 1.3 concatenate.4
  229.4 49.3 %all-gather.2 = bf16[32,12,576]{2,1,0:T(8,128)(2,1)S(1)} all-gather(bf16[1,12,576]{2,1,0:T(8,128)(2,1)S(1)} %fusion.31), channel_id=1, replica_groups=mesh['mp'=2,'tok'=8,'lat'=32] {'lat'}, dimensions={0}, use_global_device_ids=true | all-gather | bytes 456192 | tf_op jit(solution)/shard_map/all_gather | solution.py:48
  278.7 0.2 reshape.10
  279.0 1.1 fusion.14
  280.1 0.0 all-gather.6.cloned.1.call-update
  280.1 0.0 all-reduce.6.cloned.1.call-start
  280.1 106.3 %all-gather.6.cloned.1.call-done = f32[6144,256]{1,0:T(8,128)} async-done(((f32[384,256]{1,0:T(8,128)}), f32[6144,256]{1,0:T(8,128)}) %all-gather.6.cloned.1.call-update) | async-done | bytes 6291472 | tf_op jit(solution)/shard_map/all_gather | solution.py:50
  386.4 3.3 reduce_sum.9
  389.7 0.0 copy-start.6
  389.7 0.3 fusion.12
  390.1 59.5 %fusion.1 = f32[16,576]{1,0:T(8,128)S(1)} fusion(f32[384,576]{1,0:T(8,128)S(1)} %fusion.12), kind=kCustom, calls=%all-reduce-scatter.1 | all-reduce-scatter fusion | flops 294913 | bytes 923648
  449.5 1.3 collective-permute-start.10
  450.8 2.7 collective-permute-start.11
  453.6 7.5 %collective-permute-start.15 = (f32[12,576]{1,0:T(8,128)S(1)}, f32[12,576]{1,0:T(8,128)S(1)}, u32[]{:S(2)}, u32[]{:S(2)}) collective-permute-start(f32[12,576]{1,0:T(8,128)S(1)} %slice.11), channel_id=1, source_target_pairs={{0,8},{1,9},{2,10},{3,11},{4,12},{5,13},{6,14},{7,15},{8,16},{9,17... | collective-permute-start | bytes 82952
  461.1 4.8 collective-permute-start.12
  465.9 4.2 collective-permute-start.13
  470.1 2.2 collective-permute-start.14
  472.3 3.1 collective-permute-start.8
  475.4 0.0 collective-permute-done.11
  475.4 2.2 collective-permute-start.9
  477.7 0.0 collective-permute-done.13
  477.7 1.0 collective-permute-done.9
  478.7 1.0 concatenate.5
  479.8 48.9 %all-gather.3 = bf16[32,12,576]{2,1,0:T(8,128)(2,1)S(1)} all-gather(bf16[1,12,576]{2,1,0:T(8,128)(2,1)S(1)} %get-tuple-element.18), channel_id=1, replica_groups=mesh['mp'=2,'tok'=8,'lat'=32] {'lat'}, dimensions={0}, use_global_device_ids=true | all-gather | bytes 456192 | tf_op jit(solution)/shard_map/all_gather | solution.py:62
  528.7 0.2 reshape.12
  529.0 1.1 fusion.10
  530.0 0.0 all-reduce.6.cloned.1.call-update
  530.0 0.6 copy.24
  530.7 1.2 convolution_bitcast_fusion
  531.9 175.6 %all-reduce.6.cloned.1.call-done = f32[384,256]{1,0:T(8,128)} async-done(((f32[384,256]{1,0:T(8,128)}), f32[384,256]{1,0:T(8,128)}) %all-reduce.6.cloned.1.call-update) | async-done | bytes 393232 | tf_op jit(solution)/shard_map/psum | solution.py:64
  707.4 1.8 copy.28
  (23 shorter events, 0.1 us)
Async XLA Ops:
  7.2 63.5 %copy-start = (bf16[1,576,576]{2,1,0:T(8,128)(2,1)S(1)}, bf16[1,576,576]{2,1,0:T(8,128)(2,1)}, u32[]{:S(2)}) copy-start(bf16[1,576,576]{2,1,0:T(8,128)(2,1)} %param.10) | copy-start | bytes 1990660
  7.2 114.6 %reduce-scatter.8.cloned.1.call-start = ((), (), s32[]{:S(2)}) async-start(), calls=%async_computation.3 | async-start | bytes 1990656 | tf_op jit(solution)/shard_map/reduce_scatter | solution.py:26
  70.0 1.3 copy-start.2
  74.0 64.2 %copy-start.3 = (bf16[1,576,576]{2,1,0:T(8,128)(2,1)S(1)}, bf16[1,576,576]{2,1,0:T(8,128)(2,1)}, u32[]{:S(2)}) copy-start(bf16[1,576,576]{2,1,0:T(8,128)(2,1)} %param.11) | copy-start | bytes 1990660
  74.1 312.3 %all-gather.6.cloned.1.call-start = ((), (), s32[]{:S(2)}) async-start(), calls=%async_computation.2 | async-start | bytes 6684672 | tf_op jit(solution)/shard_map/all_gather | solution.py:50
  138.8 140.2 %copy-start.4 = (bf16[1,576,256]{2,1,0:T(8,128)(2,1)S(1)}, bf16[1,576,256]{2,1,0:T(8,128)(2,1)}, u32[]{:S(2)}) copy-start(bf16[1,576,256]{2,1,0:T(8,128)(2,1)} %param.12) | copy-start | bytes 884740
  197.8 22.0 %collective-permute-start = (bf16[16,576]{1,0:T(8,128)(2,1)S(1)}, bf16[16,576]{1,0:T(8,128)(2,1)S(1)}, u32[]{:S(2)}, u32[]{:S(2)}) collective-permute-start(bf16[16,576]{1,0:T(8,128)(2,1)S(1)} %convert.14), channel_id=1, source_target_pairs={{0,1},{1,2},{2,3},{3,4},{4,5},{5,6},{6,7},{7,8},{8,9},{9,10},{10,1... | collective-permute-start | bytes 55304
  199.8 23.4 %collective-permute-start.1 = (bf16[16,576]{1,0:T(8,128)(2,1)S(1)}, bf16[16,576]{1,0:T(8,128)(2,1)S(1)}, u32[]{:S(2)}, u32[]{:S(2)}) collective-permute-start(bf16[16,576]{1,0:T(8,128)(2,1)S(1)} %convert.14), channel_id=1, source_target_pairs={{0,2},{1,3},{2,4},{3,5},{4,6},{5,7},{6,8},{7,9},{8,10},{9,11},{10,... | collective-permute-start | bytes 55304
  201.6 16.0 %collective-permute-start.7 = (bf16[12,576]{1,0:T(8,128)(2,1)S(1)}, bf16[12,576]{1,0:T(8,128)(2,1)S(1)}, u32[]{:S(2)}, u32[]{:S(2)}) collective-permute-start(bf16[12,576]{1,0:T(8,128)(2,1)S(1)} %slice.10), channel_id=1, source_target_pairs={{0,8},{1,9},{2,10},{3,11},{4,12},{5,13},{6,14},{7,15},{8,16},{9,17... | collective-permute-start | bytes 41480
  207.4 20.6 %collective-permute-start.2 = (bf16[16,576]{1,0:T(8,128)(2,1)S(1)}, bf16[16,576]{1,0:T(8,128)(2,1)S(1)}, u32[]{:S(2)}, u32[]{:S(2)}) collective-permute-start(bf16[16,576]{1,0:T(8,128)(2,1)S(1)} %convert.14), channel_id=1, source_target_pairs={{0,3},{1,4},{2,5},{3,6},{4,7},{5,8},{6,9},{7,10},{8,11},{9,12},{10... | collective-permute-start | bytes 55304
  212.5 15.5 %collective-permute-start.3 = (bf16[16,576]{1,0:T(8,128)(2,1)S(1)}, bf16[16,576]{1,0:T(8,128)(2,1)S(1)}, u32[]{:S(2)}, u32[]{:S(2)}) collective-permute-start(bf16[16,576]{1,0:T(8,128)(2,1)S(1)} %convert.14), channel_id=1, source_target_pairs={{0,4},{1,5},{2,6},{3,7},{4,8},{5,9},{6,10},{7,11},{8,12},{9,13},{1... | collective-permute-start | bytes 55304
  217.7 10.4 %collective-permute-start.4 = (bf16[16,576]{1,0:T(8,128)(2,1)S(1)}, bf16[16,576]{1,0:T(8,128)(2,1)S(1)}, u32[]{:S(2)}, u32[]{:S(2)}) collective-permute-start(bf16[16,576]{1,0:T(8,128)(2,1)S(1)} %convert.14), channel_id=1, source_target_pairs={{0,5},{1,6},{2,7},{3,8},{4,9},{5,10},{6,11},{7,12},{8,13},{9,14},{... | collective-permute-start | bytes 55304
  219.8 8.2 %collective-permute-start.5 = (bf16[16,576]{1,0:T(8,128)(2,1)S(1)}, bf16[16,576]{1,0:T(8,128)(2,1)S(1)}, u32[]{:S(2)}, u32[]{:S(2)}) collective-permute-start(bf16[16,576]{1,0:T(8,128)(2,1)S(1)} %convert.14), channel_id=1, source_target_pairs={{0,6},{1,7},{2,8},{3,9},{4,10},{5,11},{6,12},{7,13},{8,14},{9,15},... | collective-permute-start | bytes 55304
  223.2 4.8 collective-permute-start.6
  280.1 427.3 %all-reduce.6.cloned.1.call-start = ((), (), s32[]{:S(2)}) async-start(), calls=%async_computation.1 | async-start | bytes 786432 | tf_op jit(solution)/shard_map/psum | solution.py:64
  386.4 3.3 copy-start.1
  386.4 3.3 copy-start.5
  389.7 87.9 %copy-start.6 = (f32[1,576]{1,0:T(1,128)S(1)}, f32[1,576]{1,0:T(1,128)}, u32[]{:S(2)}) copy-start(f32[1,576]{1,0:T(1,128)} %param.15) | copy-start | bytes 6916
  449.5 22.8 %collective-permute-start.10 = (f32[16,576]{1,0:T(8,128)S(1)}, f32[16,576]{1,0:T(8,128)S(1)}, u32[]{:S(2)}, u32[]{:S(2)}) collective-permute-start(f32[16,576]{1,0:T(8,128)S(1)} %fusion.1), channel_id=1, source_target_pairs={{0,3},{1,4},{2,5},{3,6},{4,7},{5,8},{6,9},{7,10},{8,11},{9,12},{10... | collective-permute-start | bytes 110600
  450.8 24.6 %collective-permute-start.11 = (f32[16,576]{1,0:T(8,128)S(1)}, f32[16,576]{1,0:T(8,128)S(1)}, u32[]{:S(2)}, u32[]{:S(2)}) collective-permute-start(f32[16,576]{1,0:T(8,128)S(1)} %fusion.1), channel_id=1, source_target_pairs={{0,4},{1,5},{2,6},{3,7},{4,8},{5,9},{6,10},{7,11},{8,12},{9,13},{1... | collective-permute-start | bytes 110600
  453.6 16.5 %collective-permute-start.15 = (f32[12,576]{1,0:T(8,128)S(1)}, f32[12,576]{1,0:T(8,128)S(1)}, u32[]{:S(2)}, u32[]{:S(2)}) collective-permute-start(f32[12,576]{1,0:T(8,128)S(1)} %slice.11), channel_id=1, source_target_pairs={{0,8},{1,9},{2,10},{3,11},{4,12},{5,13},{6,14},{7,15},{8,16},{9,17... | collective-permute-start | bytes 82952
  461.1 16.6 %collective-permute-start.12 = (f32[16,576]{1,0:T(8,128)S(1)}, f32[16,576]{1,0:T(8,128)S(1)}, u32[]{:S(2)}, u32[]{:S(2)}) collective-permute-start(f32[16,576]{1,0:T(8,128)S(1)} %fusion.1), channel_id=1, source_target_pairs={{0,5},{1,6},{2,7},{3,8},{4,9},{5,10},{6,11},{7,12},{8,13},{9,14},{... | collective-permute-start | bytes 110600
  465.9 11.8 %collective-permute-start.13 = (f32[16,576]{1,0:T(8,128)S(1)}, f32[16,576]{1,0:T(8,128)S(1)}, u32[]{:S(2)}, u32[]{:S(2)}) collective-permute-start(f32[16,576]{1,0:T(8,128)S(1)} %fusion.1), channel_id=1, source_target_pairs={{0,6},{1,7},{2,8},{3,9},{4,10},{5,11},{6,12},{7,13},{8,14},{9,15},... | collective-permute-start | bytes 110600
  470.1 7.6 %collective-permute-start.14 = (f32[16,576]{1,0:T(8,128)S(1)}, f32[16,576]{1,0:T(8,128)S(1)}, u32[]{:S(2)}, u32[]{:S(2)}) collective-permute-start(f32[16,576]{1,0:T(8,128)S(1)} %fusion.1), channel_id=1, source_target_pairs={{0,7},{1,8},{2,9},{3,10},{4,11},{5,12},{6,13},{7,14},{8,15},{9,16}... | collective-permute-start | bytes 110600
  472.3 5.4 collective-permute-start.8
  475.4 3.3 collective-permute-start.9
Sparse Core Ops, SparseCore 0:
  74.2 47.5 reduce-scatter.7
  280.2 106.1 all-gather.5
  530.2 177.2 all-reduce.5
